TPU v7x, 256 devices: a whole 4x4x8 slice. The times are simulated.
256 devices in a mesh: replica: 32 (over x_lo, z, core), tensor: 8 (over y, x_hi).
Axes of the slice: x: 4 (x_hi: 2, x_lo: 2; x = x_hi * 2 + x_lo), y: 4, z: 8, core: 2. Of those that a mesh axis runs over, the one named last changes fastest.
Arguments:
- inputs: bfloat16 [2, 16384, 2048], P(None, 'replica', 'tensor'), may hold values from -6 to 6
- out_grads: bfloat16 [2, 16384, 2048], P(None, 'replica', 'tensor'), may hold values from -6 to 6
- gate_weight: bfloat16 [32, 2048, 2816], P('replica', None, 'tensor'), may hold values from -0.125 to 0.125
- up_weight: bfloat16 [32, 2048, 2816], P('replica', None, 'tensor'), may hold values from -0.125 to 0.125
- down_weight: bfloat16 [32, 2816, 2048], P('replica', 'tensor'), may hold values from -0.109375 to 0.109375
- rates: float32 [32], P('replica'), may hold values from 16 to 64
- partner_bits: int32 [4], replicated, may hold values from 0 to 3, each once
Outputs:
- new_gate: bfloat16 [32, 2048, 2816], P('replica', None, 'tensor')
- new_up: bfloat16 [32, 2048, 2816], P('replica', None, 'tensor')
- new_down: bfloat16 [32, 2816, 2048], P('replica', 'tensor')
- activations: bfloat16 [2, 16384, 2048], P(None, 'replica', 'tensor')
Inputs may be any that keep to these rules, and one draw needn't show every extreme that they name: partner_bits holds each of the bit numbers 0, 1, 2, 3 exactly once; step s uses entry s.
All inputs are finite; a program needn't handle non-finite values.
Results may differ from a plain program's by a relative error of at most 0.024.
Values may be sent and summed in bfloat16 or wider, within the bound.
No kernel may reach another device: no remote copies, remote signals or barrier semaphores. Data moves between devices by JAX's collectives and lax.ppermute only.
A program may use at most 128 MiB of HBM per device.

v0:
```python
from functools import partial
import jax
import jax.numpy as jnp
from jax import lax
from jax.sharding import PartitionSpec as P


def shortened(value):

    def short(part):
        return part.astype(jnp.bfloat16) if part.dtype == jnp.float32 else part

    return jax.tree.map(short, value)


def partner(value, axis, distance):
    mask = 2**distance
    pairs = [(source, source ^ mask) for source in range(lax.axis_size(axis))]
    return lax.ppermute(value, axis, pairs)


def local_pass(weights, inputs, grads_out):
    gate_w, up_w, down_w = weights
    gate = jnp.dot(inputs, gate_w, preferred_element_type=jnp.float32)
    up = jnp.dot(inputs, up_w, preferred_element_type=jnp.float32)
    sigma = jax.nn.sigmoid(gate)
    active = gate * sigma
    hidden = (active * up).astype(jnp.bfloat16)
    mixed = jnp.dot(hidden, down_w, preferred_element_type=jnp.float32)
    back = lax.dot_general(
        grads_out, down_w, (((1,), (1,)), ((), ())), preferred_element_type=jnp.float32
    )
    d_gate = (back * up * sigma * (1.0 + gate * (1.0 - sigma))).astype(jnp.bfloat16)
    d_up = (back * active).astype(jnp.bfloat16)
    grad_down = lax.dot_general(
        hidden, grads_out, (((0,), (0,)), ((), ())), preferred_element_type=jnp.float32
    )
    grad_gate = lax.dot_general(
        inputs, d_gate, (((0,), (0,)), ((), ())), preferred_element_type=jnp.float32
    )
    grad_up = lax.dot_general(
        inputs, d_up, (((0,), (0,)), ((), ())), preferred_element_type=jnp.float32
    )
    return (mixed, (grad_gate, grad_up, grad_down))


def squares_of(grads):
    return sum((jnp.sum(g * g) for g in grads))


def apply_update(weights, grads, squares, rate):
    scale = rate / jnp.sqrt(squares + 1e-06)
    return tuple(
        ((w.astype(jnp.float32) - scale * g).astype(jnp.bfloat16) for w, g in zip(weights, grads))
    )


def average(first, second):
    return tuple(
        (
            ((a.astype(jnp.float32) + b.astype(jnp.float32)) * 0.5).astype(jnp.bfloat16)
            for a, b in zip(first, second)
        )
    )


def total_norms(values):
    return lax.psum((values[0],), "tensor")


def mixing_bit(bit_number, values):
    return jax.tree.map(
        lambda piece: jax.tree.map(
            lambda part, own: part.astype(own.dtype),
            partner(shortened(piece), "replica", bit_number),
            piece,
        ),
        values,
    )


def partner_values(values, bit, handler):
    branches = [partial(handler, number) for number in range(4)]
    return lax.switch(bit, branches, values)


def local(inputs, out_grads, gate_weight, up_weight, down_weight, rates, partner_bits):
    weights = (gate_weight[0], up_weight[0], down_weight[0])
    results = []
    for step in range(inputs.shape[0]):
        whole_x, whole_dy = (
            lax.all_gather(inputs[step], "tensor", axis=1, tiled=True),
            lax.all_gather(out_grads[step], "tensor", axis=1, tiled=True),
        )
        bit = partner_bits[step]
        mixed, grads = local_pass(weights, whole_x, whole_dy)
        squares = total_norms((squares_of(grads),))[0]
        fresh = apply_update(weights, grads, squares, rates[0])
        other = partner_values(fresh, bit, mixing_bit)
        weights = average(fresh, other)
        summed = lax.psum_scatter(
            mixed.astype(jnp.bfloat16), "tensor", scatter_dimension=1, tiled=True
        )
        results.append(summed)
    return (weights[0][None], weights[1][None], weights[2][None], jnp.stack(results))


def solution(mesh):
    return jax.shard_map(
        local,
        mesh=mesh,
        in_specs=(
            P(None, "replica", "tensor"),
            P(None, "replica", "tensor"),
            P("replica", None, "tensor"),
            P("replica", None, "tensor"),
            P("replica", "tensor", None),
            P("replica"),
            P(),
        ),
        out_specs=(
            P("replica", None, "tensor"),
            P("replica", None, "tensor"),
            P("replica", "tensor", None),
            P(None, "replica", "tensor"),
        ),
        check_vma=False,
    )
```

profile of v0, /device:TPU:32, one launch (start us, length us, event | category | flops | bytes accessed | tf_op | source)
XLA Modules:
  0.0 427.8 jit_solution(12777738690879736687)
XLA Ops:
  13.8 59.1 %all-gather.11.cloned.1.call-done = bf16[1,512,2048]{2,1,0:T(8,128)(2,1)} async-done(((bf16[1,512,256]{2,1,0:T(8,128)(2,1)}), bf16[1,512,2048]{2,1,0:T(8,128)(2,1)}) %all-gather.11.cloned.1.call-update) | async-done | bytes 2097168 | tf_op jit(solution)/shard_map/all_gather | solution.py:92
  80.2 52.8 %all-gather.9.cloned.1.call-done = bf16[1,512,2048]{2,1,0:T(8,128)(2,1)} async-done(((bf16[1,512,256]{2,1,0:T(8,128)(2,1)}), bf16[1,512,2048]{2,1,0:T(8,128)(2,1)}) %all-gather.9.cloned.1.call-update) | async-done | bytes 2097168 | tf_op jit(solution)/shard_map/all_gather | solution.py:93
  135.7 3.2 multiply_reduce_fusion.4
  138.9 3.3 multiply_reduce_fusion.5
  143.5 3.2 multiply_reduce_fusion.3
  147.9 20.4 %psum.14 = f32[]{:T(128)} all-reduce(f32[]{:T(128)S(6)} %add.59), channel_id=1, replica_groups=mesh['replica'=32,'tensor'=8] {'tensor'}, use_global_device_ids=true, to_apply=%region_3.0 | all-reduce | flops 1 | bytes 8 | tf_op jit(solution)/shard_map/psum | solution.py:68
  175.0 90.9 %conditional.8 = (bf16[2048,352]{0,1:T(8,128)(2,1)}, bf16[352,2048]{1,0:T(8,128)(2,1)}, bf16[2048,352]{0,1:T(8,128)(2,1)}) conditional(s32[]{:T(128)} %bitcast.7, (bf16[2048,352]{0,1:T(8,128)(2,1)S(1)}, bf16[2048,352]{0,1:T(8,128)(2,1)S(1)}, bf16[352,2048]{1,0:T(8,128)(2,1)S(1)}) %tuple.108, ...), branch_computations={%region_4.0_spmd, %region_5.0_spmd, %region_6.0_spmd, %region_7.0_... | conditional | bytes 17301648
  177.6 32.1 %collective-permute-done.3 = bf16[2048,352]{0,1:T(8,128)(2,1)} collective-permute-done((bf16[2048,352]{0,1:T(8,128)(2,1)S(1)}, bf16[2048,352]{0,1:T(8,128)(2,1)}, u32[]{:S(2)}, u32[]{:S(2)}) %collective-permute-start.3) | collective-permute-done | bytes 1441824 | tf_op jit(solution)/shard_map/cond/branch_1_fun/ppermute | solution.py:19
  209.7 30.9 %collective-permute-done.4 = bf16[2048,352]{0,1:T(8,128)(2,1)} collective-permute-done((bf16[2048,352]{0,1:T(8,128)(2,1)S(1)}, bf16[2048,352]{0,1:T(8,128)(2,1)}, u32[]{:S(2)}, u32[]{:S(2)}) %collective-permute-start.4) | collective-permute-done | bytes 1441824 | tf_op jit(solution)/shard_map/cond/branch_1_fun/ppermute | solution.py:19
  240.6 25.3 %collective-permute-done.5 = bf16[352,2048]{1,0:T(8,128)(2,1)} collective-permute-done((bf16[352,2048]{1,0:T(8,128)(2,1)S(1)}, bf16[352,2048]{1,0:T(8,128)(2,1)}, u32[]{:S(2)}, u32[]{:S(2)}) %collective-permute-start.5) | collective-permute-done | bytes 1441824 | tf_op jit(solution)/shard_map/cond/branch_1_fun/ppermute | solution.py:19
  265.9 3.1 fusion.53
  269.1 3.5 multiply_convert_fusion
  272.6 4.0 convolution_convert_fusion
  276.6 3.2 fusion.47
  279.9 3.1 multiply_reduce_fusion.1
  283.0 3.3 multiply_reduce_fusion.2
  287.5 3.2 multiply_reduce_fusion
  292.0 22.9 %psum.15 = f32[]{:T(128)} all-reduce(f32[]{:T(128)S(6)} %add.67), channel_id=1, replica_groups=mesh['replica'=32,'tensor'=8] {'tensor'}, use_global_device_ids=true, to_apply=%region_11.0 | all-reduce | flops 1 | bytes 8 | tf_op jit(solution)/shard_map/psum | solution.py:68
  319.0 4.4 %fusion.12 = (bf16[2048,352]{0,1:T(8,128)(2,1)S(1)}, bf16[2048,352]{0,1:T(8,128)(2,1)S(1)}) fusion(f32[352,2048]{1,0:T(8,128)S(1)} %copy-done.10, f32[]{:T(128)S(6)} %div.15, bf16[2048,352]{0,1:T(8,128)(2,1)} %get-tuple-element.159, bf16[2048,352]{0,1:T(8,128)(2,1)S(1)} %copy-done.5, f32[352,2048]{1,0:T(8,128)} %get-tuple-element.181, ...), kind=kLoop, calls=%fused_computation.21 | loop fusion | flops 12976128 | bytes 14417924 | tf_op jit(solution)/shard_map/convert_element_type | solution.py:54
  323.5 7.6 %conditional.9 = (bf16[2048,352]{0,1:T(8,128)(2,1)}, bf16[2048,352]{0,1:T(8,128)(2,1)}, bf16[352,2048]{1,0:T(8,128)(2,1)}) conditional(s32[]{:T(128)} %bitcast.15, (bf16[2048,352]{0,1:T(8,128)(2,1)S(1)}, bf16[2048,352]{0,1:T(8,128)(2,1)S(1)}, bf16[352,2048]{1,0:T(8,128)(2,1)S(1)}) %tuple.109, ...), branch_computations={%region_12.0_spmd, %region_13.0_spmd, %region_14.0_spmd, %region_1... | conditional | bytes 17301648
  331.0 3.1 fusion.40
  334.1 3.0 fusion.42
  337.1 3.0 fusion.41
  340.1 79.1 %reduce-scatter.5.cloned.1.call-done = bf16[512,256]{1,0:T(8,128)(2,1)} async-done(((bf16[512,2048]{1,0:T(8,128)(2,1)}), bf16[512,256]{1,0:T(8,128)(2,1)}) %reduce-scatter.5.cloned.1.call-update) | async-done | bytes 262160 | tf_op jit(solution)/shard_map/reduce_scatter | solution.py:101
  (90 shorter events, 37.4 us)
Async XLA Ops:
  7.2 6.0 %copy-start.16 = (s32[4]{0:T(128)S(1)}, s32[4]{0:T(128)}, u32[]{:S(2)}) copy-start(s32[4]{0:T(128)} %param.21) | copy-start | bytes 52
  7.2 65.7 %copy-start.14 = (bf16[1,2048,352]{1,2,0:T(8,128)(2,1)S(1)}, bf16[1,2048,352]{1,2,0:T(8,128)(2,1)}, u32[]{:S(2)}) copy-start(bf16[1,2048,352]{1,2,0:T(8,128)(2,1)} %param.17) | copy-start | bytes 4325380
  7.2 65.6 %all-gather.11.cloned.1.call-start = ((), (), s32[]{:S(2)}) async-start(), calls=%async_computation.5 | async-start | bytes 2359296 | tf_op jit(solution)/shard_map/all_gather | solution.py:92
  9.2 123.7 %all-gather.9.cloned.1.call-start = ((), (), s32[]{:S(2)}) async-start(), calls=%async_computation.4 | async-start | bytes 2359296 | tf_op jit(solution)/shard_map/all_gather | solution.py:93
  11.2 254.7 %all-gather.15.cloned.1.call-start = ((), (), s32[]{:S(2)}) async-start(), calls=%async_computation.7 | async-start | bytes 2359296 | tf_op jit(solution)/shard_map/all_gather | solution.py:92
  11.9 264.7 %all-gather.13.cloned.1.call-start = ((), (), s32[]{:S(2)}) async-start(), calls=%async_computation.6 | async-start | bytes 2359296 | tf_op jit(solution)/shard_map/all_gather | solution.py:93
  12.5 327.6 %reduce-scatter.3.cloned.1.call-start = ((), (), s32[]{:S(2)}) async-start(), calls=%async_computation.2 | async-start | bytes 2359296 | tf_op jit(solution)/shard_map/reduce_scatter | solution.py:101
  13.8 61.8 %copy-start.12 = (bf16[1,2048,352]{1,2,0:T(8,128)(2,1)S(1)}, bf16[1,2048,352]{1,2,0:T(8,128)(2,1)}, u32[]{:S(2)}) copy-start(bf16[1,2048,352]{1,2,0:T(8,128)(2,1)} %param.18) | copy-start | bytes 4325380
  80.2 55.5 %copy-start.22 = (f32[512,352]{0,1:T(8,128)S(1)}, f32[512,352]{0,1:T(8,128)}, u32[]{:S(2)}) copy-start(f32[512,352]{0,1:T(8,128)} %copy-done.21) | copy-start | bytes 2162692
  80.2 338.9 %reduce-scatter.5.cloned.1.call-start = ((), (), s32[]{:S(2)}) async-start(), calls=%async_computation.3 | async-start | bytes 2359296 | tf_op jit(solution)/shard_map/reduce_scatter | solution.py:101
  171.1 3.9 copy-start.2
  172.2 96.9 %copy-start.4 = (bf16[2048,352]{0,1:T(8,128)(2,1)}, bf16[2048,352]{0,1:T(8,128)(2,1)S(1)}, u32[]{:S(2)}) copy-start(bf16[2048,352]{0,1:T(8,128)(2,1)S(1)} %fusion.14) | copy-start | bytes 4325380
  175.0 94.0 %copy-start.6 = (bf16[2048,352]{0,1:T(8,128)(2,1)}, bf16[2048,352]{0,1:T(8,128)(2,1)S(1)}, u32[]{:S(2)}) copy-start(bf16[2048,352]{0,1:T(8,128)(2,1)S(1)} %fusion.15) | copy-start | bytes 4325380
  175.0 34.6 %collective-permute-start.3 = (bf16[2048,352]{0,1:T(8,128)(2,1)S(1)}, bf16[2048,352]{0,1:T(8,128)(2,1)}, u32[]{:S(2)}, u32[]{:S(2)}) collective-permute-start(bf16[2048,352]{0,1:T(8,128)(2,1)S(1)} %get-tuple-element.87), channel_id=1, source_target_pairs={{0,16},{8,24},{16,0},{24,8},{32,48},{40,56},{48,32},{56,40},{64,80... | collective-permute-start | bytes 4325384 | tf_op jit(solution)/shard_map/cond/branch_1_fun/ppermute | solution.py:19
  175.6 65.0 %collective-permute-start.4 = (bf16[2048,352]{0,1:T(8,128)(2,1)S(1)}, bf16[2048,352]{0,1:T(8,128)(2,1)}, u32[]{:S(2)}, u32[]{:S(2)}) collective-permute-start(bf16[2048,352]{0,1:T(8,128)(2,1)S(1)} %get-tuple-element.88), channel_id=1, source_target_pairs={{0,16},{8,24},{16,0},{24,8},{32,48},{40,56},{48,32},{56,40},{64,80... | collective-permute-start | bytes 4325384 | tf_op jit(solution)/shard_map/cond/branch_1_fun/ppermute | solution.py:19
  177.2 88.7 %collective-permute-start.5 = (bf16[352,2048]{1,0:T(8,128)(2,1)S(1)}, bf16[352,2048]{1,0:T(8,128)(2,1)}, u32[]{:S(2)}, u32[]{:S(2)}) collective-permute-start(bf16[352,2048]{1,0:T(8,128)(2,1)S(1)} %get-tuple-element.89), channel_id=1, source_target_pairs={{0,16},{8,24},{16,0},{24,8},{32,48},{40,56},{48,32},{56,40},{64,80... | collective-permute-start | bytes 4325384 | tf_op jit(solution)/shard_map/cond/branch_1_fun/ppermute | solution.py:19
  269.0 3.5 copy-start.23
  269.1 3.5 copy-start.3
  276.6 3.2 copy-start.24
  315.5 3.5 copy-start.10
  318.2 5.3 %copy-start = (bf16[352,2048]{1,0:T(8,128)(2,1)}, bf16[352,2048]{1,0:T(8,128)(2,1)S(1)}, u32[]{:S(2)}) copy-start(bf16[352,2048]{1,0:T(8,128)(2,1)S(1)} %subtract_convert_fusion) | copy-start | bytes 4325380
  323.5 3.4 collective-permute-start.12
  323.6 5.4 %collective-permute-start.13 = (bf16[2048,352]{0,1:T(8,128)(2,1)S(1)}, bf16[2048,352]{0,1:T(8,128)(2,1)}, u32[]{:S(2)}, u32[]{:S(2)}) collective-permute-start(bf16[2048,352]{0,1:T(8,128)(2,1)S(1)} %get-tuple-element.97), channel_id=1, source_target_pairs={{0,8},{8,0},{16,24},{24,16},{32,40},{40,32},{48,56},{56,48},{64,72... | collective-permute-start | bytes 4325384 | tf_op jit(solution)/shard_map/cond/branch_0_fun/ppermute | solution.py:19
  324.1 7.0 %collective-permute-start.14 = (bf16[352,2048]{1,0:T(8,128)(2,1)S(1)}, bf16[352,2048]{1,0:T(8,128)(2,1)}, u32[]{:S(2)}, u32[]{:S(2)}) collective-permute-start(bf16[352,2048]{1,0:T(8,128)(2,1)S(1)} %get-tuple-element.98), channel_id=1, source_target_pairs={{0,8},{8,0},{16,24},{24,16},{32,40},{40,32},{48,56},{56,48},{64,72... | collective-permute-start | bytes 4325384 | tf_op jit(solution)/shard_map/cond/branch_0_fun/ppermute | solution.py:19
  (15 other events, 40.6 us)
Sparse Core Ops, SparseCore 0:
  11.0 61.7 all-gather.10
  75.9 57.0 all-gather.8
  135.5 57.1 all-gather.14
  195.0 57.0 all-gather.12
  255.9 79.1 reduce-scatter.2
  339.0 80.0 reduce-scatter.4
where the time goes:
time: 428 us
  waiting for transfers between devices  287 us (67%)
  blocking collectives  43.2 us (10%)
  matrix products  43 us (10%)
  between operations  21.5 us (5%)
  other arithmetic  20.9 us (5%)
  local copies, waits for them, and re-layouts  8.34 us (2%)
    ppermute x6, waiting for transfers between devices, partner(): return lax.ppermute(value, axis, pairs)  95.1 us
    reduce_scatter x2, waiting for transfers between devices, local(): lax.psum_scatter(mixed.astype(jnp.bfloat16), 'tensor', scatter_dimension=...  79.1 us
    all_gather x2, waiting for transfers between devices, local(): lax.all_gather(inputs[step], 'tensor', axis=1, tiled=True)  59.1 us
    all_gather x2, waiting for transfers between devices, local(): lax.all_gather(out_grads[step], 'tensor', axis=1, tiled=True)  52.8 us
    psum x2, blocking collectives, total_norms(): return lax.psum((values[0],), 'tensor')  43.2 us
    convert_element_type x5, other arithmetic, apply_update(): (w.astype(jnp.float32) - scale * g).astype(jnp.bfloat16)  10 us
  transfers between devices with their start and end apart: 12, of which 9 were waited for; matrix products, arithmetic and copies ran while one was open for 15% of the time, Pallas kernels for 0%

commit v1 on v0

--- a/solution.py
+++ b/solution.py
@@ -89,7 +89,10 @@
     results = []
     for step in range(inputs.shape[0]):
         whole_x, whole_dy = (
-            lax.all_gather(inputs[step], "tensor", axis=1, tiled=True),
+            jnp.concatenate(
+                lax.all_to_all(jnp.stack([inputs[step]] * lax.axis_size("tensor")), "tensor", 0, 0),
+                axis=1,
+            ),
             lax.all_gather(out_grads[step], "tensor", axis=1, tiled=True),
         )
         bit = partner_bits[step]

time: 428 us -> 335 us (0.78)
  waiting for transfers between devices: 287 us -> 180 us
  starting transfers between devices: 3.52 us -> 14.6 us
    reduce_scatter x2, waiting for transfers between devices: 79.1 us -> 17.5 us  [local(): lax.psum_scatter(mixed.astype(jnp.bfloat16), 'tensor', scatter_dimension=...]
    all_gather x2 -> x0, waiting for transfers between devices: 59.1 us -> none  [local(): lax.all_gather(inputs[step], 'tensor', axis=1, tiled=True)]
    all_to_all x0 -> x2, waiting for transfers between devices: none -> 29.9 us  [local(): lax.all_to_all(jnp.stack([inputs[step]] * lax.axis_size('tensor')), 'tens...]
    all_gather x2, waiting for transfers between devices: 52.8 us -> 35.1 us  [local(): lax.all_gather(out_grads[step], 'tensor', axis=1, tiled=True)]
    all_to_all x0 -> x2, starting transfers between devices: none -> 11.6 us  [local(): lax.all_to_all(jnp.stack([inputs[step]] * lax.axis_size('tensor')), 'tens...]
  transfers between devices with their start and end apart: 12 -> 12, of which waited for: 9 -> 9; matrix products, arithmetic and copies ran while one was open for 15% -> 20% of each run, Pallas kernels for 0% -> 0%
where the time goes in v1:
time: 335 us; the launch traced here: 334 us
  waiting for transfers between devices  180 us (54%)
  matrix products  43 us (13%)
  blocking collectives  42.7 us (13%)
  between operations  21.1 us (6%)
  other arithmetic  20.7 us (6%)
  starting transfers between devices  14.6 us (4%)
  local copies, waits for them, and re-layouts  11.9 us (4%)
    ppermute x6, waiting for transfers between devices, partner(): return lax.ppermute(value, axis, pairs)  96.6 us
    psum x2, blocking collectives, total_norms(): return lax.psum((values[0],), 'tensor')  42.7 us
    all_gather x2, waiting for transfers between devices, local(): lax.all_gather(out_grads[step], 'tensor', axis=1, tiled=True)  35.1 us
    all_to_all x2, waiting for transfers between devices, local(): lax.all_to_all(jnp.stack([inputs[step]] * lax.axis_size('tensor')), 'tens...  29.9 us
    reduce_scatter x2, waiting for transfers between devices, local(): lax.psum_scatter(mixed.astype(jnp.bfloat16), 'tensor', scatter_dimension=...  17.5 us
    all_to_all x2, starting transfers between devices, local(): lax.all_to_all(jnp.stack([inputs[step]] * lax.axis_size('tensor')), 'tens...  11.6 us
    convert_element_type x5, other arithmetic, apply_update(): (w.astype(jnp.float32) - scale * g).astype(jnp.bfloat16)  9.86 us
    dot_general x2, matrix products, local_pass(): lax.dot_general(inputs, d_gate, (((0,), (0,)), ((), ())), preferred_eleme...  8.11 us
  transfers between devices with their start and end apart: 12, of which 9 were waited for; matrix products, arithmetic and copies ran while one was open for 20% of the time, Pallas kernels for 0%

profile of v1, /device:TPU:32, one launch (start us, length us, event | category | flops | bytes accessed | tf_op | source)
XLA Modules:
  0.0 334.1 jit_solution(11968677122626932629)
XLA Ops:
  12.6 7.1 %all-to-all-start = ((bf16[8,512,256]{1,2,0:T(8,128)(2,1)}), bf16[8,512,256]{1,2,0:T(8,128)(2,1)S(1)}, u32[]{:S(2)}, u32[]{:S(2)}) async-start(bf16[8,512,256]{1,2,0:T(8,128)(2,1)} %stack.15), calls=%async_computation | async-start | bytes 4194304 | tf_op jit(solution)/shard_map/all_to_all | solution.py:93
  21.1 29.9 %all-to-all-done = bf16[8,512,256]{1,2,0:T(8,128)(2,1)S(1)} async-done(((bf16[8,512,256]{1,2,0:T(8,128)(2,1)}), bf16[8,512,256]{1,2,0:T(8,128)(2,1)S(1)}, u32[]{:S(2)}, u32[]{:S(2)}) %all-to-all-start) | async-done | bytes 2097184 | tf_op jit(solution)/shard_map/all_to_all | solution.py:93
  52.5 4.5 %all-to-all-start.1 = ((bf16[8,512,256]{1,2,0:T(8,128)(2,1)}), bf16[8,512,256]{1,2,0:T(8,128)(2,1)}, u32[]{:S(2)}, u32[]{:S(2)}) async-start(bf16[8,512,256]{1,2,0:T(8,128)(2,1)} %stack.16), calls=%async_computation.1 | async-start | bytes 4194304 | tf_op jit(solution)/shard_map/all_to_all | solution.py:93
  63.7 35.1 %all-gather.5.cloned.1.call-done = bf16[1,512,2048]{2,1,0:T(8,128)(2,1)} async-done(((bf16[1,512,256]{2,1,0:T(8,128)(2,1)}), bf16[1,512,2048]{2,1,0:T(8,128)(2,1)}) %all-gather.5.cloned.1.call-update) | async-done | bytes 2097168 | tf_op jit(solution)/shard_map/all_gather | solution.py:96
  101.4 3.1 multiply_reduce_fusion.4
  104.6 3.2 multiply_reduce_fusion.5
  112.0 20.0 %psum.14 = f32[]{:T(128)} all-reduce(f32[]{:T(128)S(6)} %add.59), channel_id=1, replica_groups=mesh['replica'=32,'tensor'=8] {'tensor'}, use_global_device_ids=true, to_apply=%region_3.0 | all-reduce | flops 1 | bytes 8 | tf_op jit(solution)/shard_map/psum | solution.py:68
  138.6 92.0 %conditional.8 = (bf16[2048,352]{0,1:T(8,128)(2,1)}, bf16[352,2048]{1,0:T(8,128)(2,1)}, bf16[2048,352]{0,1:T(8,128)(2,1)}) conditional(s32[]{:T(128)} %bitcast.10, (bf16[2048,352]{0,1:T(8,128)(2,1)S(1)}, bf16[2048,352]{0,1:T(8,128)(2,1)S(1)}, bf16[352,2048]{1,0:T(8,128)(2,1)S(1)}) %tuple.108, ...), branch_computations={%region_4.0_spmd, %region_5.0_spmd, %region_6.0_spmd, %region_7.0_... | conditional | bytes 17301648
  140.9 32.4 %collective-permute-done.3 = bf16[2048,352]{0,1:T(8,128)(2,1)} collective-permute-done((bf16[2048,352]{0,1:T(8,128)(2,1)S(1)}, bf16[2048,352]{0,1:T(8,128)(2,1)}, u32[]{:S(2)}, u32[]{:S(2)}) %collective-permute-start.3) | collective-permute-done | bytes 1441824 | tf_op jit(solution)/shard_map/cond/branch_1_fun/ppermute | solution.py:19
  173.3 30.9 %collective-permute-done.4 = bf16[2048,352]{0,1:T(8,128)(2,1)} collective-permute-done((bf16[2048,352]{0,1:T(8,128)(2,1)S(1)}, bf16[2048,352]{0,1:T(8,128)(2,1)}, u32[]{:S(2)}, u32[]{:S(2)}) %collective-permute-start.4) | collective-permute-done | bytes 1441824 | tf_op jit(solution)/shard_map/cond/branch_1_fun/ppermute | solution.py:19
  204.2 26.4 %collective-permute-done.5 = bf16[352,2048]{1,0:T(8,128)(2,1)} collective-permute-done((bf16[352,2048]{1,0:T(8,128)(2,1)S(1)}, bf16[352,2048]{1,0:T(8,128)(2,1)}, u32[]{:S(2)}, u32[]{:S(2)}) %collective-permute-start.5) | collective-permute-done | bytes 1441824 | tf_op jit(solution)/shard_map/cond/branch_1_fun/ppermute | solution.py:19
  233.6 4.1 %multiply_convert_fusion = (bf16[512,352]{0,1:T(8,128)(2,1)S(1)}, f32[512,352]{0,1:T(8,128)}) fusion(f32[512,352]{0,1:T(8,128)S(1)} %convolution_bitcast_fusion, bf16[512,2048]{0,1:T(8,128)(2,1)} %bitcast.16, bf16[2048,352]{0,1:T(8,128)(2,1)} %get-tuple-element.183, bf16[2048,352]{0,1:T(8,128)(2,1)S(1)} %fusion.14), kind=kOutput, calls=%fused_computation.56 | convolution fusion | flops 742883328 | bytes 6782976 | tf_op jit(solution)/shard_map/dot_general | solution.py:25
  237.7 4.0 %convolution_convert_fusion = bf16[512,2048]{1,0:T(8,128)(2,1)} fusion(bf16[512,352]{0,1:T(8,128)(2,1)S(1)} %get-tuple-element.208, bf16[352,2048]{1,0:T(8,128)(2,1)} %get-tuple-element.182, bf16[352,2048]{1,0:T(8,128)(2,1)S(1)} %copy-done.3), kind=kOutput, calls=%fused_computation | convolution fusion | flops 742850560 | bytes 5341184 | tf_op jit(solution)/shard_map/dot_general | solution.py:29
  241.8 3.0 fusion.33
  244.9 4.8 %multiply_reduce_fusion.1 = (f32[]{:T(128)}, f32[352,2048]{1,0:T(8,128)}) fusion(bf16[512,2048]{0,1:T(8,128)(2,1)} %bitcast.16, f32[512,352]{0,1:T(8,128)S(1)} %fusion.33, f32[512,352]{0,1:T(8,128)S(1)} %copy-done.21), kind=kOutput, calls=%fused_computation.30 | convolution fusion | flops 740720640 | bytes 6422532 | tf_op jit(solution)/shard_map/dot_general | solution.py:41
  249.7 4.9 %multiply_reduce_fusion.2 = (f32[]{:T(128)}, f32[352,2048]{1,0:T(8,128)}) fusion(bf16[512,2048]{0,1:T(8,128)(2,1)} %bitcast.16, f32[512,352]{0,1:T(8,128)S(1)} %copy-done.21, f32[512,352]{0,1:T(8,128)S(1)} %fusion.33, f32[512,352]{0,1:T(8,128)S(1)} %copy-done.25), kind=kOutput, calls=%fused_computation.31 | convolution fusion | flops 741441536 | bytes 7143428 | tf_op jit(solution)/shard_map/dot_general | solution.py:38
  255.8 3.3 multiply_reduce_fusion
  260.3 22.8 %psum.15 = f32[]{:T(128)} all-reduce(f32[]{:T(128)S(6)} %add.67), channel_id=1, replica_groups=mesh['replica'=32,'tensor'=8] {'tensor'}, use_global_device_ids=true, to_apply=%region_11.0 | all-reduce | flops 1 | bytes 8 | tf_op jit(solution)/shard_map/psum | solution.py:68
  287.3 4.2 %fusion.12 = (bf16[2048,352]{0,1:T(8,128)(2,1)S(1)}, bf16[2048,352]{0,1:T(8,128)(2,1)S(1)}) fusion(f32[352,2048]{1,0:T(8,128)S(1)} %copy-done.10, f32[]{:T(128)S(6)} %div.15, bf16[2048,352]{0,1:T(8,128)(2,1)} %get-tuple-element.183, bf16[2048,352]{0,1:T(8,128)(2,1)S(1)} %copy-done.5, f32[352,2048]{1,0:T(8,128)} %get-tuple-element.205, ...), kind=kLoop, calls=%fused_computation.21 | loop fusion | flops 12976128 | bytes 14417924 | tf_op jit(solution)/shard_map/convert_element_type | solution.py:54
  291.6 7.6 %conditional.9 = (bf16[2048,352]{0,1:T(8,128)(2,1)}, bf16[2048,352]{0,1:T(8,128)(2,1)}, bf16[352,2048]{1,0:T(8,128)(2,1)}) conditional(s32[]{:T(128)} %bitcast.21, (bf16[2048,352]{0,1:T(8,128)(2,1)S(1)}, bf16[2048,352]{0,1:T(8,128)(2,1)S(1)}, bf16[352,2048]{1,0:T(8,128)(2,1)S(1)}) %tuple.109, ...), branch_computations={%region_12.0_spmd, %region_13.0_spmd, %region_14.0_spmd, %region_1... | conditional | bytes 17301648
  299.2 3.1 fusion.24
  302.2 3.0 fusion.26
  305.2 3.0 fusion.25
  308.2 17.5 %reduce-scatter.5.cloned.1.call-done = bf16[512,256]{1,0:T(8,128)(2,1)} async-done(((bf16[512,2048]{1,0:T(8,128)(2,1)}), bf16[512,256]{1,0:T(8,128)(2,1)}) %reduce-scatter.5.cloned.1.call-update) | async-done | bytes 262160 | tf_op jit(solution)/shard_map/reduce_scatter | solution.py:104
  (90 shorter events, 42.6 us)
Async XLA Ops:
  7.2 91.6 %all-gather.5.cloned.1.call-start = ((), (), s32[]{:S(2)}) async-start(), calls=%async_computation.6 | async-start | bytes 2359296 | tf_op jit(solution)/shard_map/all_gather | solution.py:96
  9.1 232.7 %all-gather.7.cloned.1.call-start = ((), (), s32[]{:S(2)}) async-start(), calls=%async_computation.7 | async-start | bytes 2359296 | tf_op jit(solution)/shard_map/all_gather | solution.py:96
  12.6 7.9 %copy-start.19 = (s32[4]{0:T(128)S(1)}, s32[4]{0:T(128)}, u32[]{:S(2)}) copy-start(s32[4]{0:T(128)} %param.21) | copy-start | bytes 52
  12.6 38.4 %all-to-all-start = ((bf16[8,512,256]{1,2,0:T(8,128)(2,1)}), bf16[8,512,256]{1,2,0:T(8,128)(2,1)S(1)}, u32[]{:S(2)}, u32[]{:S(2)}) async-start(bf16[8,512,256]{1,2,0:T(8,128)(2,1)} %stack.15), calls=%async_computation | async-start | bytes 4194304 | tf_op jit(solution)/shard_map/all_to_all | solution.py:93
  52.5 4.6 %copy-start.15 = (bf16[1,2048,352]{1,2,0:T(8,128)(2,1)S(1)}, bf16[1,2048,352]{1,2,0:T(8,128)(2,1)}, u32[]{:S(2)}) copy-start(bf16[1,2048,352]{1,2,0:T(8,128)(2,1)} %param.17) | copy-start | bytes 4325380
  52.5 178.1 %all-to-all-start.1 = ((bf16[8,512,256]{1,2,0:T(8,128)(2,1)}), bf16[8,512,256]{1,2,0:T(8,128)(2,1)}, u32[]{:S(2)}, u32[]{:S(2)}) async-start(bf16[8,512,256]{1,2,0:T(8,128)(2,1)} %stack.16), calls=%async_computation.1 | async-start | bytes 4194304 | tf_op jit(solution)/shard_map/all_to_all | solution.py:93
  57.0 251.1 %reduce-scatter.3.cloned.1.call-start = ((), (), s32[]{:S(2)}) async-start(), calls=%async_computation.4 | async-start | bytes 2359296 | tf_op jit(solution)/shard_map/reduce_scatter | solution.py:104
  63.6 262.0 %reduce-scatter.5.cloned.1.call-start = ((), (), s32[]{:S(2)}) async-start(), calls=%async_computation.5 | async-start | bytes 2359296 | tf_op jit(solution)/shard_map/reduce_scatter | solution.py:104
  104.6 3.3 copy-start.11
  104.6 3.3 copy-start.18
  134.7 3.9 %copy-start.2 = (bf16[352,2048]{1,0:T(8,128)(2,1)}, bf16[352,2048]{1,0:T(8,128)(2,1)S(1)}, u32[]{:S(2)}) copy-start(bf16[352,2048]{1,0:T(8,128)(2,1)S(1)} %subtract_convert_fusion.1) | copy-start | bytes 4325380
  135.8 97.8 %copy-start.4 = (bf16[2048,352]{0,1:T(8,128)(2,1)}, bf16[2048,352]{0,1:T(8,128)(2,1)S(1)}, u32[]{:S(2)}) copy-start(bf16[2048,352]{0,1:T(8,128)(2,1)S(1)} %fusion.14) | copy-start | bytes 4325380
  138.6 94.9 %copy-start.6 = (bf16[2048,352]{0,1:T(8,128)(2,1)}, bf16[2048,352]{0,1:T(8,128)(2,1)S(1)}, u32[]{:S(2)}) copy-start(bf16[2048,352]{0,1:T(8,128)(2,1)S(1)} %fusion.15) | copy-start | bytes 4325380
  138.7 34.6 %collective-permute-start.3 = (bf16[2048,352]{0,1:T(8,128)(2,1)S(1)}, bf16[2048,352]{0,1:T(8,128)(2,1)}, u32[]{:S(2)}, u32[]{:S(2)}) collective-permute-start(bf16[2048,352]{0,1:T(8,128)(2,1)S(1)} %get-tuple-element.87), channel_id=1, source_target_pairs={{0,16},{8,24},{16,0},{24,8},{32,48},{40,56},{48,32},{56,40},{64,80... | collective-permute-start | bytes 4325384 | tf_op jit(solution)/shard_map/cond/branch_1_fun/ppermute | solution.py:19
  138.8 65.4 %collective-permute-start.4 = (bf16[2048,352]{0,1:T(8,128)(2,1)S(1)}, bf16[2048,352]{0,1:T(8,128)(2,1)}, u32[]{:S(2)}, u32[]{:S(2)}) collective-permute-start(bf16[2048,352]{0,1:T(8,128)(2,1)S(1)} %get-tuple-element.88), channel_id=1, source_target_pairs={{0,16},{8,24},{16,0},{24,8},{32,48},{40,56},{48,32},{56,40},{64,80... | collective-permute-start | bytes 4325384 | tf_op jit(solution)/shard_map/cond/branch_1_fun/ppermute | solution.py:19
  140.8 89.8 %collective-permute-start.5 = (bf16[352,2048]{1,0:T(8,128)(2,1)S(1)}, bf16[352,2048]{1,0:T(8,128)(2,1)}, u32[]{:S(2)}, u32[]{:S(2)}) collective-permute-start(bf16[352,2048]{1,0:T(8,128)(2,1)S(1)} %get-tuple-element.89), channel_id=1, source_target_pairs={{0,16},{8,24},{16,0},{24,8},{32,48},{40,56},{48,32},{56,40},{64,80... | collective-permute-start | bytes 4325384 | tf_op jit(solution)/shard_map/cond/branch_1_fun/ppermute | solution.py:19
  233.6 4.2 %copy-start.20 = (f32[512,352]{0,1:T(8,128)}, f32[512,352]{0,1:T(8,128)S(1)}, u32[]{:S(2)}) copy-start(f32[512,352]{0,1:T(8,128)S(1)} %convolution_bitcast_fusion) | copy-start | bytes 2162692
  233.6 4.1 %copy-start.3 = (bf16[352,2048]{1,0:T(8,128)(2,1)S(1)}, bf16[352,2048]{1,0:T(8,128)(2,1)}, u32[]{:S(2)}) copy-start(bf16[352,2048]{1,0:T(8,128)(2,1)} %copy-done.2) | copy-start | bytes 4325380
  244.9 4.8 %copy-start.25 = (f32[512,352]{0,1:T(8,128)S(1)}, f32[512,352]{0,1:T(8,128)}, u32[]{:S(2)}) copy-start(f32[512,352]{0,1:T(8,128)} %get-tuple-element.209) | copy-start | bytes 2162692
  283.8 3.6 %copy-start.10 = (f32[352,2048]{1,0:T(8,128)S(1)}, f32[352,2048]{1,0:T(8,128)}, u32[]{:S(2)}) copy-start(f32[352,2048]{1,0:T(8,128)} %get-tuple-element.207) | copy-start | bytes 8650756
  286.4 5.1 %copy-start = (bf16[352,2048]{1,0:T(8,128)(2,1)}, bf16[352,2048]{1,0:T(8,128)(2,1)S(1)}, u32[]{:S(2)}) copy-start(bf16[352,2048]{1,0:T(8,128)(2,1)S(1)} %subtract_convert_fusion) | copy-start | bytes 4325380
  291.6 3.4 %collective-permute-start.12 = (bf16[2048,352]{0,1:T(8,128)(2,1)S(1)}, bf16[2048,352]{0,1:T(8,128)(2,1)}, u32[]{:S(2)}, u32[]{:S(2)}) collective-permute-start(bf16[2048,352]{0,1:T(8,128)(2,1)S(1)} %get-tuple-element.96), channel_id=1, source_target_pairs={{0,8},{8,0},{16,24},{24,16},{32,40},{40,32},{48,56},{56,48},{64,72... | collective-permute-start | bytes 4325384 | tf_op jit(solution)/shard_map/cond/branch_0_fun/ppermute | solution.py:19
  291.7 5.4 %collective-permute-start.13 = (bf16[2048,352]{0,1:T(8,128)(2,1)S(1)}, bf16[2048,352]{0,1:T(8,128)(2,1)}, u32[]{:S(2)}, u32[]{:S(2)}) collective-permute-start(bf16[2048,352]{0,1:T(8,128)(2,1)S(1)} %get-tuple-element.97), channel_id=1, source_target_pairs={{0,8},{8,0},{16,24},{24,16},{32,40},{40,32},{48,56},{56,48},{64,72... | collective-permute-start | bytes 4325384 | tf_op jit(solution)/shard_map/cond/branch_0_fun/ppermute | solution.py:19
  292.2 7.0 %collective-permute-start.14 = (bf16[352,2048]{1,0:T(8,128)(2,1)S(1)}, bf16[352,2048]{1,0:T(8,128)(2,1)}, u32[]{:S(2)}, u32[]{:S(2)}) collective-permute-start(bf16[352,2048]{1,0:T(8,128)(2,1)S(1)} %get-tuple-element.98), channel_id=1, source_target_pairs={{0,8},{8,0},{16,24},{24,16},{32,40},{40,32},{48,56},{56,48},{64,72... | collective-permute-start | bytes 4325384 | tf_op jit(solution)/shard_map/cond/branch_0_fun/ppermute | solution.py:19
  (14 other events, 33.8 us)
Sparse Core Ops, SparseCore 0:
  11.0 87.7 all-gather.4
  101.3 57.1 all-gather.6
  162.5 79.1 reduce-scatter.2
  245.6 80.0 reduce-scatter.4
